TPU v7x, 128 devices: a whole 4x4x4 slice. The times are simulated.
128 devices in a mesh: leaf: 2 (over core), front: 64 (over z, y, x).
Axes of the slice: x: 4, y: 4, z: 4, core: 2. Of those that a mesh axis runs over, the one named last changes fastest.
Arguments:
- front_block: float32 [8192, 8192], P('leaf', 'front'), as said below
- child_update: float32 [2, 6144, 8192], P('leaf', None, 'front'), as said below
- child_map: int32 [2, 48], P('leaf'), may hold values from 0 to 63, as said below
Outputs:
- factored: float32 [8192, 8192], P('leaf', 'front')
Inputs may be any that keep to these rules, and one draw needn't show every extreme that they name: `child_map`: each row is strictly increasing, holds 48 distinct blocks, and always names block 0 and block 63. `front_block`: Symmetric; the assembled front is positive definite. `child_update`: each child's update is symmetric and positive semidefinite in the child's order; columns of parent blocks that the child's map does not name are zero.
All inputs are finite; a program needn't handle non-finite values.
Results may differ from a plain program's by a relative error of at most 0.000088.
Values sent between devices are 32-bit elements; how exact they have to be, the bound alone decides.
A program may use at most 128 MiB of HBM per device.

v0:
```python
import jax
import jax.numpy as jnp
from jax import lax
from jax.sharding import PartitionSpec as P

BLK = 128
S = 512
HIGHEST = lax.Precision.HIGHEST


def gather_half(blocks, child_map, half, half_blocks):
    parent = half * half_blocks + jnp.arange(half_blocks, dtype=jnp.int32)
    hit = child_map[None, :] == parent[:, None]
    found = jnp.any(hit, axis=1)
    index = jnp.argmax(hit, axis=1)
    picked = jnp.take(blocks, index, axis=0)
    picked = jnp.where(found[:, None, None], picked, jnp.zeros_like(picked))
    return picked.reshape(half_blocks * BLK, blocks.shape[2])


def per_device(front_block, child_update, child_map):
    rows, cols = front_block.shape
    n_leaf = lax.axis_size("leaf")
    n_front = lax.axis_size("front")
    leaf = lax.axis_index("leaf")
    front = lax.axis_index("front")
    half_blocks = rows // BLK
    blocks = child_update[0].reshape(-1, BLK, cols)
    cmap = child_map[0]
    own = gather_half(blocks, cmap, leaf, half_blocks)
    send = gather_half(blocks, cmap, 1 - leaf, half_blocks)
    recv = lax.ppermute(send, "leaf", [(0, 1), (1, 0)])
    first = jnp.where(leaf == 0, own, recv)
    second = jnp.where(leaf == 0, recv, own)
    assembled = front_block + first + second
    top = assembled[:S]
    piv_cols = S // cols
    is_piv = front < piv_cols
    col_at = jnp.minimum(front, piv_cols - 1) * cols
    panel = lax.dynamic_update_slice_in_dim(
        jnp.zeros((S, S), jnp.float32), jnp.where(is_piv, top, jnp.zeros_like(top)), col_at, 1
    )
    pivot = lax.psum(panel, "front")
    factor = jnp.linalg.cholesky(pivot)
    own_solved = lax.linalg.triangular_solve(factor, top, left_side=True, lower=True).T
    from_leaf0 = lax.ppermute(own_solved, "leaf", [(0, 1)])
    col_solved = jnp.where(leaf == 0, own_solved, from_leaf0)
    piece = rows // n_front
    per_block = BLK // piece
    pieces = []
    for part in range(per_block):
        pairs = []
        for lf in range(n_leaf):
            for k in range(n_front // per_block):
                src = lf * n_front + lf * half_blocks + k
                dst = lf * n_front + per_block * k + part
                pairs.append((src, dst))
        pieces.append(
            lax.ppermute(col_solved[part * piece : (part + 1) * piece], ("leaf", "front"), pairs)
        )
    my_piece = pieces[0]
    for part in range(1, per_block):
        my_piece = jnp.where(front % per_block == part, pieces[part], my_piece)
    row_solved = lax.all_gather(my_piece, "front", tiled=True)
    schur = assembled - jnp.dot(row_solved, col_solved.T, precision=HIGHEST)
    row_global = leaf * rows + jnp.arange(rows, dtype=jnp.int32)
    col_global = front * cols + jnp.arange(cols, dtype=jnp.int32)
    col_start = jnp.minimum(front * cols, S - cols)
    left_rows = lax.dynamic_slice_in_dim(row_solved, col_start, cols, 1)
    left_top = jnp.pad(
        lax.dynamic_slice_in_dim(factor, col_start, cols, 1), ((0, rows - S), (0, 0))
    )
    left_part = jnp.where(row_global[:, None] < S, left_top, left_rows)
    right_top = jnp.pad(col_solved.T, ((0, rows - S), (0, 0)))
    right_part = jnp.where(row_global[:, None] < S, right_top, schur)
    return jnp.where(col_global[None, :] < S, left_part, right_part)


def solution(mesh):
    return jax.shard_map(
        per_device,
        mesh=mesh,
        in_specs=(P("leaf", "front"), P("leaf", None, "front"), P("leaf", None)),
        out_specs=P("leaf", "front"),
        check_vma=False,
    )
```

profile of v0, /device:TPU:1, one launch (start us, length us, event | category | flops | bytes accessed | tf_op | source)
XLA Modules:
  0.0 471.3 jit_solution(12014427817205239228)
XLA Ops:
  10.3 2.0 gather_fusion.1
  12.3 3.2 select_select_fusion
  15.5 2.9 copy.84
  19.9 2.0 gather_fusion
  21.8 3.2 select_select_fusion.1
  25.1 2.9 copy.83
  28.0 2.9 copy.56
  30.8 3.3 select_add_fusion
  37.1 129.3 %all-reduce.5.cloned.1.call-done = f32[512,512]{0,1:T(8,128)} async-done(((f32[512,512]{0,1:T(8,128)}), f32[512,512]{0,1:T(8,128)}) %all-reduce.5.cloned.1.call-update) | async-done | bytes 1048592 | tf_op jit(solution)/shard_map/psum | solution.py:43
  166.4 2.6 copy.57
  171.8 11.7 %cholesky.103 = f32[128,128]{1,0:T(8,128)S(1)} custom-call(f32[128,128]{1,0:T(8,128)S(1)} %cholesky.263), custom_call_target="Cholesky" | custom-call | tf_op jit(solution)/shard_map/jit(cholesky)/cholesky | solution.py:44
  184.3 9.8 %custom-call.30 = f32[1,128,128]{1,2,0:T(8,128)S(1)} custom-call(f32[1,128,128]{2,1,0:T(8,128)S(1)} %get-tuple-element.55), custom_call_target="InvertDiagBlocksLowerTriangular" | custom-call | tf_op jit(solution)/shard_map/jit(cholesky)/cholesky | solution.py:44
  195.3 1.9 convolution_subtract_fusion.1
  198.9 13.2 %cholesky.215 = f32[128,128]{1,0:T(8,128)} custom-call(f32[128,128]{1,0:T(8,128)} %cholesky.267), custom_call_target="Cholesky" | custom-call | tf_op jit(solution)/shard_map/jit(cholesky)/cholesky | solution.py:44
  215.1 11.4 %custom-call.31 = f32[1,128,128]{1,2,0:T(8,128)} custom-call(f32[1,128,128]{2,1,0:T(8,128)} %get-tuple-element.53), custom_call_target="InvertDiagBlocksLowerTriangular" | custom-call | tf_op jit(solution)/shard_map/jit(cholesky)/cholesky | solution.py:44
  232.1 11.7 %cholesky.236 = f32[128,128]{1,0:T(8,128)S(1)} custom-call(f32[128,128]{1,0:T(8,128)S(1)} %cholesky.272), custom_call_target="Cholesky" | custom-call | tf_op jit(solution)/shard_map/jit(cholesky)/cholesky | solution.py:44
  244.6 9.8 %custom-call.32 = f32[1,128,128]{1,2,0:T(8,128)S(1)} custom-call(f32[1,128,128]{2,1,0:T(8,128)S(1)} %get-tuple-element.51), custom_call_target="InvertDiagBlocksLowerTriangular" | custom-call | tf_op jit(solution)/shard_map/jit(cholesky)/cholesky | solution.py:44
  256.8 11.9 %cholesky.253 = f32[128,128]{1,0:T(8,128)S(1)} custom-call(f32[128,128]{1,0:T(8,128)S(1)} %convolution_subtract_fusion.3), custom_call_target="Cholesky" | custom-call | tf_op jit(solution)/shard_map/jit(cholesky)/cholesky | solution.py:44
  276.3 14.5 %while.1 = (s32[]{:T(128)}, f32[512,512]{0,1:T(8,128)}, s32[4,2]{0,1:T(2,128)S(1)}, f32[4,128,128]{2,1,0:T(8,128)}, s32[]{:T(128)}) while((s32[]{:T(128)}, f32[512,512]{0,1:T(8,128)}, s32[4,2]{0,1:T(2,128)S(1)}, f32[4,128,128]{2,1,0:T(8,128)}, s32[]{:T(128)}) %tuple.35), condition=%wide.while_cond, body=%wide.while_body.sunk | while | flops 2 | bytes 393329 | solution.py:45
  277.0 2.2 dynamic-slice.7
  280.6 2.2 dynamic-slice.7
  284.3 2.2 dynamic-slice.7
  287.9 2.2 dynamic-slice.7
  290.8 40.1 %custom-call.33 = f32[4,128,128]{1,2,0:T(8,128)S(1)} custom-call(f32[4,128,128]{2,1,0:T(8,128)} %get-tuple-element.17), custom_call_target="InvertDiagBlocksLowerTriangular" | custom-call | tf_op jit(solution)/shard_map/triangular_solve | solution.py:45
  337.8 2.0 fusion.4
  342.4 4.9 %collective-permute-done.1 = f32[128,512]{1,0:T(8,128)S(1)} collective-permute-done((f32[128,512]{1,0:T(8,128)S(1)}, f32[128,512]{1,0:T(8,128)S(1)}, u32[]{:S(2)}, u32[]{:S(2)}) %collective-permute-start.1) | collective-permute-done | bytes 262176 | tf_op jit(solution)/shard_map/ppermute | solution.py:46
  351.4 4.8 %collective-permute-done.3 = f32[64,512]{1,0:T(8,128)S(1)} collective-permute-done((f32[64,512]{1,0:T(8,128)}, f32[64,512]{1,0:T(8,128)S(1)}, u32[]{:S(2)}, u32[]{:S(2)}) %collective-permute-start.3) | collective-permute-done | bytes 131104 | tf_op jit(solution)/shard_map/ppermute | solution.py:59
  358.7 80.8 %all-gather.2.cloned.1.call-done = f32[4096,512]{1,0:T(8,128)} async-done(((f32[64,512]{1,0:T(8,128)}), f32[4096,512]{1,0:T(8,128)}) %all-gather.2.cloned.1.call-update) | async-done | bytes 8388624 | tf_op jit(solution)/shard_map/all_gather | solution.py:64
  439.5 4.2 constant_dynamic-slice_fusion.1
  443.7 2.9 copy.86
  446.6 14.8 %select_select_fusion.2 = f32[4096,128]{0,1:T(8,128)} fusion(f32[512,128]{0,1:T(8,128)S(1)} %bitcast.58, f32[4096,128]{0,1:T(8,128)} %copy.86, f32[512,128]{0,1:T(8,128)} %constant_dynamic-slice_fusion.2, pred[128]{0:T(512)(128)(4,1)S(1)} %add_compare_fusion.1, pred[4096]{0:T(1024)(128)(4,1)S(1)} %add_compare_fusion, f32[4096,128]{0,1:T(8,128)} %copy-done.1, ...), kind=kOutput, calls=%fused_computation.7 | convolution fusion | flops 3223322624 | bytes 15470720 | tf_op jit(solution)/shard_map/dot_general | solution.py:65
  461.4 2.9 copy.75
  (98 shorter events, 52.7 us)
Async XLA Ops:
  6.5 3.8 copy-start
  6.5 159.9 %all-reduce.5.cloned.1.call-start = ((), (), s32[]{:S(2)}) async-start(), calls=%async_computation | async-start | bytes 2097152 | tf_op jit(solution)/shard_map/psum | solution.py:43
  18.4 12.4 %collective-permute-start = (f32[4096,128]{0,1:T(8,128)}, f32[4096,128]{0,1:T(8,128)}, u32[]{:S(2)}, u32[]{:S(2)}) collective-permute-start(f32[4096,128]{0,1:T(8,128)} %copy.84), channel_id=1, source_target_pairs={{0,64},{64,0},{1,65},{65,1},{2,66},{66,2},{3,67},{67,3},{4,68},{68... | collective-permute-start | bytes 6291464 | tf_op jit(solution)/shard_map/ppermute | solution.py:32
  34.1 1.7 copy-start.1
  36.6 403.0 %all-gather.2.cloned.1.call-start = ((), (), s32[]{:S(2)}) async-start(), calls=%async_computation.1 | async-start | bytes 8519680 | tf_op jit(solution)/shard_map/all_gather | solution.py:64
  170.8 1.0 copy-start.3
  197.4 31.0 %copy-start.4 = (f32[384,128]{1,0:T(8,128)S(1)}, f32[384,128]{1,0:T(8,128)}, u32[]{:S(2)}) copy-start(f32[384,128]{1,0:T(8,128)} %convolution_subtract_fusion.1) | copy-start | bytes 589828
  229.5 1.0 copy-start.2
  331.0 0.7 copy-start.6
  339.9 2.5 copy-start.5
  341.1 6.2 %collective-permute-start.1 = (f32[128,512]{1,0:T(8,128)S(1)}, f32[128,512]{1,0:T(8,128)S(1)}, u32[]{:S(2)}, u32[]{:S(2)}) collective-permute-start(f32[128,512]{1,0:T(8,128)S(1)} %maximum_bitcast_fusion), channel_id=1, source_target_pairs={{0,64},{1,65},{2,66},{3,67},{4,68},{5,69},{6,70},{7,71},{8,72},{9,... | collective-permute-start | bytes 786440 | tf_op jit(solution)/shard_map/ppermute | solution.py:46
  348.8 7.4 %collective-permute-start.3 = (f32[64,512]{1,0:T(8,128)}, f32[64,512]{1,0:T(8,128)S(1)}, u32[]{:S(2)}, u32[]{:S(2)}) collective-permute-start(f32[64,512]{1,0:T(8,128)} %get-tuple-element.48), channel_id=1, source_target_pairs={{0,0},{1,2},{2,4},{3,6},{4,8},{5,10},{6,12},{7,14},{8,16},{9,18},{... | collective-permute-start | bytes 393224 | tf_op jit(solution)/shard_map/ppermute | solution.py:59
  350.1 6.1 %collective-permute-start.2 = (f32[64,512]{1,0:T(8,128)}, f32[64,512]{1,0:T(8,128)}, u32[]{:S(2)}, u32[]{:S(2)}) collective-permute-start(f32[64,512]{1,0:T(8,128)} %get-tuple-element.49), channel_id=1, source_target_pairs={{0,1},{1,3},{2,5},{3,7},{4,9},{5,11},{6,13},{7,15},{8,17},{9,19},{... | collective-permute-start | bytes 393224 | tf_op jit(solution)/shard_map/ppermute | solution.py:59
Sparse Core Ops, SparseCore 0:
  36.7 129.7 all-reduce.4
  357.1 82.4 all-gather.1
where the time goes:
time: 476 us; the launch traced here: 471 us
  waiting for transfers between devices  220 us (46%)
  other arithmetic  143 us (30%)
  local copies, waits for them, and re-layouts  54 us (11%)
  matrix products  32.1 us (7%)
  between operations  16.5 us (3%)
  starting transfers between devices  5.81 us (1%)
    psum x1, waiting for transfers between devices, per_device(): pivot = lax.psum(panel, 'front')  129 us
    another operation x15, other arithmetic, per_device(): factor = jnp.linalg.cholesky(pivot)  83.8 us
    all_gather x1, waiting for transfers between devices, per_device(): row_solved = lax.all_gather(my_piece, 'front', tiled=True)  80.8 us
    another operation x3, other arithmetic, per_device(): lax.linalg.triangular_solve(factor, top, left_side=True, lower=True)  41.7 us
    dot_general x1, matrix products, per_device(): schur = assembled - jnp.dot(row_solved, col_solved.T, precision=HIGHEST)  14.8 us
    another operation x20, local copies, waits for them, and re-layouts  14.5 us
  transfers between devices with their start and end apart: 6, of which 4 were waited for; matrix products, arithmetic and copies ran while one was open for 3% of the time, Pallas kernels for 0%

commit v1 on v0

--- a/solution.py
+++ b/solution.py
@@ -61,7 +61,14 @@
     my_piece = pieces[0]
     for part in range(1, per_block):
         my_piece = jnp.where(front % per_block == part, pieces[part], my_piece)
-    row_solved = lax.all_gather(my_piece, "front", tiled=True)
+
+    def recast_axis_part_by_axis(vals, peer_axis):
+        a_next = lax.all_to_all(
+            jnp.stack([vals for _ in range(lax.axis_size(peer_axis))], 0), peer_axis, 0, 0
+        )
+        return jnp.concatenate(a_next, 0)
+
+    row_solved = recast_axis_part_by_axis(my_piece, "front")
     schur = assembled - jnp.dot(row_solved, col_solved.T, precision=HIGHEST)
     row_global = leaf * rows + jnp.arange(rows, dtype=jnp.int32)
     col_global = front * cols + jnp.arange(cols, dtype=jnp.int32)

time: 476 us -> 525 us (1.10)
  the two profiles are of different devices: /device:TPU:1 before, /device:TPU:4 now
where the time goes in v1:
time: 525 us; the launch traced here: 521 us
  waiting for transfers between devices  248 us (47%)
  other arithmetic  144 us (27%)
  local copies, waits for them, and re-layouts  58.6 us (11%)
  matrix products  32.1 us (6%)
  starting transfers between devices  22 us (4%)
  between operations  16.5 us (3%)
    psum x1, waiting for transfers between devices, per_device(): pivot = lax.psum(panel, 'front')  131 us
    all_to_all x1, waiting for transfers between devices, recast_axis_part_by_axis(): lax.all_to_all(jnp.stack([vals for _ in range(lax.axis_size(peer_axis))],...  114 us
    another operation x15, other arithmetic, per_device(): factor = jnp.linalg.cholesky(pivot)  84.1 us
    another operation x3, other arithmetic, per_device(): lax.linalg.triangular_solve(factor, top, left_side=True, lower=True)  43 us
    dot_general x1, matrix products, per_device(): schur = assembled - jnp.dot(row_solved, col_solved.T, precision=HIGHEST)  14.8 us
    another operation x20, local copies, waits for them, and re-layouts  14.5 us
    all_to_all x1, starting transfers between devices, recast_axis_part_by_axis(): lax.all_to_all(jnp.stack([vals for _ in range(lax.axis_size(peer_axis))],...  13.6 us
  transfers between devices with their start and end apart: 6, of which 4 were waited for; matrix products, arithmetic and copies ran while one was open for 2% of the time, Pallas kernels for 0%

profile of v1, /device:TPU:4, one launch (start us, length us, event | category | flops | bytes accessed | tf_op | source)
XLA Modules:
  0.0 521.3 jit_solution(1699008181446185633)
XLA Ops:
  12.3 3.2 select_select_fusion
  15.5 2.9 copy.70
  20.4 3.2 select_select_fusion.1
  23.6 2.9 copy.69
  26.5 3.1 copy.42
  29.7 3.3 select_add_fusion
  35.4 130.9 %all-reduce.5.cloned.1.call-done = f32[512,512]{0,1:T(8,128)} async-done(((f32[512,512]{0,1:T(8,128)}), f32[512,512]{0,1:T(8,128)}) %all-reduce.5.cloned.1.call-update) | async-done | bytes 1048592 | tf_op jit(solution)/shard_map/psum | solution.py:43
  166.3 2.6 copy.43
  171.6 11.7 %cholesky.103 = f32[128,128]{1,0:T(8,128)S(1)} custom-call(f32[128,128]{1,0:T(8,128)S(1)} %cholesky.263), custom_call_target="Cholesky" | custom-call | tf_op jit(solution)/shard_map/jit(cholesky)/cholesky | solution.py:44
  184.1 9.8 %custom-call.30 = f32[1,128,128]{1,2,0:T(8,128)S(1)} custom-call(f32[1,128,128]{2,1,0:T(8,128)S(1)} %get-tuple-element.51), custom_call_target="InvertDiagBlocksLowerTriangular" | custom-call | tf_op jit(solution)/shard_map/jit(cholesky)/cholesky | solution.py:44
  198.8 13.2 %cholesky.215 = f32[128,128]{1,0:T(8,128)} custom-call(f32[128,128]{1,0:T(8,128)} %cholesky.267), custom_call_target="Cholesky" | custom-call | tf_op jit(solution)/shard_map/jit(cholesky)/cholesky | solution.py:44
  215.0 11.8 %custom-call.31 = f32[1,128,128]{1,2,0:T(8,128)} custom-call(f32[1,128,128]{2,1,0:T(8,128)} %get-tuple-element.49), custom_call_target="InvertDiagBlocksLowerTriangular" | custom-call | tf_op jit(solution)/shard_map/jit(cholesky)/cholesky | solution.py:44
  232.3 11.7 %cholesky.236 = f32[128,128]{1,0:T(8,128)S(1)} custom-call(f32[128,128]{1,0:T(8,128)S(1)} %cholesky.272), custom_call_target="Cholesky" | custom-call | tf_op jit(solution)/shard_map/jit(cholesky)/cholesky | solution.py:44
  244.8 9.8 %custom-call.32 = f32[1,128,128]{1,2,0:T(8,128)S(1)} custom-call(f32[1,128,128]{2,1,0:T(8,128)S(1)} %get-tuple-element.47), custom_call_target="InvertDiagBlocksLowerTriangular" | custom-call | tf_op jit(solution)/shard_map/jit(cholesky)/cholesky | solution.py:44
  257.0 11.9 %cholesky.253 = f32[128,128]{1,0:T(8,128)S(1)} custom-call(f32[128,128]{1,0:T(8,128)S(1)} %convolution_subtract_fusion.3), custom_call_target="Cholesky" | custom-call | tf_op jit(solution)/shard_map/jit(cholesky)/cholesky | solution.py:44
  274.9 2.9 fusion.1
  277.8 14.5 %while.1 = (s32[]{:T(128)}, f32[512,512]{0,1:T(8,128)}, s32[4,2]{0,1:T(2,128)S(1)}, f32[4,128,128]{2,1,0:T(8,128)}, s32[]{:T(128)}) while((s32[]{:T(128)}, f32[512,512]{0,1:T(8,128)}, s32[4,2]{0,1:T(2,128)S(1)}, f32[4,128,128]{2,1,0:T(8,128)}, s32[]{:T(128)}) %tuple.34), condition=%wide.while_cond, body=%wide.while_body.sunk | while | flops 2 | bytes 393329 | solution.py:45
  278.5 2.2 dynamic-slice.7
  282.1 2.2 dynamic-slice.7
  285.8 2.2 dynamic-slice.7
  289.4 2.2 dynamic-slice.7
  292.3 40.1 %custom-call.33 = f32[4,128,128]{1,2,0:T(8,128)S(1)} custom-call(f32[4,128,128]{2,1,0:T(8,128)} %get-tuple-element.17), custom_call_target="InvertDiagBlocksLowerTriangular" | custom-call | tf_op jit(solution)/shard_map/triangular_solve | solution.py:45
  346.6 3.6 collective-permute-start.3
  350.2 3.5 collective-permute-start.2
  353.7 2.2 collective-permute-done.2
  355.9 4.3 stack.2
  360.2 13.6 %all-to-all-start = ((f32[64,64,512]{2,1,0:T(8,128)}), f32[64,64,512]{2,1,0:T(8,128)}, u32[]{:S(2)}, u32[]{:S(2)}) async-start(f32[64,64,512]{2,1,0:T(8,128)} %stack.2), calls=%async_computation | async-start | bytes 16777216 | tf_op jit(solution)/shard_map/all_to_all | solution.py:66
  375.6 113.9 %all-to-all-done = f32[64,64,512]{2,1,0:T(8,128)} async-done(((f32[64,64,512]{2,1,0:T(8,128)}), f32[64,64,512]{2,1,0:T(8,128)}, u32[]{:S(2)}, u32[]{:S(2)}) %all-to-all-start) | async-done | bytes 8388640 | tf_op jit(solution)/shard_map/all_to_all | solution.py:66
  489.5 4.2 constant_dynamic-slice_fusion.1
  493.7 2.9 copy.72
  496.6 14.8 %select_select_fusion.2 = f32[4096,128]{0,1:T(8,128)} fusion(f32[512,128]{0,1:T(8,128)S(1)} %bitcast.59, f32[4096,128]{0,1:T(8,128)} %copy.72, f32[512,128]{0,1:T(8,128)} %constant_dynamic-slice_fusion.2, pred[128]{0:T(512)(128)(4,1)S(1)} %add_compare_fusion.1, pred[4096]{0:T(1024)(128)(4,1)S(1)} %add_compare_fusion, f32[4096,128]{0,1:T(8,128)} %copy-done.1, ...), kind=kOutput, calls=%fused_computation.7 | convolution fusion | flops 3223322624 | bytes 15470720 | tf_op jit(solution)/shard_map/dot_general | solution.py:72
  511.4 2.9 copy.61
  (98 shorter events, 55.0 us)
Async XLA Ops:
  6.5 3.8 copy-start
  6.5 159.7 %all-reduce.5.cloned.1.call-start = ((), (), s32[]{:S(2)}) async-start(), calls=%async_computation.1 | async-start | bytes 2097152 | tf_op jit(solution)/shard_map/psum | solution.py:43
  18.4 11.3 %collective-permute-start = (f32[4096,128]{0,1:T(8,128)}, f32[4096,128]{0,1:T(8,128)}, u32[]{:S(2)}, u32[]{:S(2)}) collective-permute-start(f32[4096,128]{0,1:T(8,128)} %copy.70), channel_id=1, source_target_pairs={{0,64},{64,0},{1,65},{65,1},{2,66},{66,2},{3,67},{67,3},{4,68},{68... | collective-permute-start | bytes 6291464 | tf_op jit(solution)/shard_map/ppermute | solution.py:32
  33.0 1.7 copy-start.1
  170.6 1.0 copy-start.3
  197.2 31.3 %copy-start.4 = (f32[384,128]{1,0:T(8,128)S(1)}, f32[384,128]{1,0:T(8,128)}, u32[]{:S(2)}) copy-start(f32[384,128]{1,0:T(8,128)} %convolution_subtract_fusion.1) | copy-start | bytes 589828
  229.7 1.0 copy-start.2
  332.5 0.7 copy-start.6
  341.4 2.5 copy-start.5
  342.6 2.4 collective-permute-start.1
  346.6 7.1 %collective-permute-start.3 = (f32[64,512]{1,0:T(8,128)}, f32[64,512]{1,0:T(8,128)S(1)}, u32[]{:S(2)}, u32[]{:S(2)}) collective-permute-start(f32[64,512]{1,0:T(8,128)} %get-tuple-element.44), channel_id=1, source_target_pairs={{0,0},{1,2},{2,4},{3,6},{4,8},{5,10},{6,12},{7,14},{8,16},{9,18},{... | collective-permute-start | bytes 393224 | tf_op jit(solution)/shard_map/ppermute | solution.py:59
  350.2 5.7 %collective-permute-start.2 = (f32[64,512]{1,0:T(8,128)}, f32[64,512]{1,0:T(8,128)}, u32[]{:S(2)}, u32[]{:S(2)}) collective-permute-start(f32[64,512]{1,0:T(8,128)} %get-tuple-element.45), channel_id=1, source_target_pairs={{0,1},{1,3},{2,5},{3,7},{4,9},{5,11},{6,13},{7,15},{8,17},{9,19},{... | collective-permute-start | bytes 393224 | tf_op jit(solution)/shard_map/ppermute | solution.py:59
  360.2 129.3 %all-to-all-start = ((f32[64,64,512]{2,1,0:T(8,128)}), f32[64,64,512]{2,1,0:T(8,128)}, u32[]{:S(2)}, u32[]{:S(2)}) async-start(f32[64,64,512]{2,1,0:T(8,128)} %stack.2), calls=%async_computation | async-start | bytes 16777216 | tf_op jit(solution)/shard_map/all_to_all | solution.py:66
Sparse Core Ops, SparseCore 0:
  35.5 130.7 all-reduce.4
